TPU v7x, 32 devices: a whole 2x2x4 slice. The times are simulated.
32 devices in a mesh: depth: 2 (over y), row: 4 (over z), col: 4 (over x, core).
Axes of the slice: x: 2, y: 2, z: 4, core: 2. Of those that a mesh axis runs over, the one named last changes fastest.
Arguments:
- prop: bfloat16 [2, 2, 8192, 8192], P('depth', None, 'row', 'col'), may hold values from -0.046875 to 0.046875
- source: float32 [8192, 256], P(('row', 'col')), may hold values from -6 to 6
- down_init: float32 [2, 8192, 256], P('depth', ('row', 'col')), may hold values from -6 to 6
- up_init: float32 [2, 8192, 256], P('depth', ('row', 'col')), may hold values from -6 to 6
- refl_down: float32 [2, 8192], P('depth', ('row', 'col')), may hold values from -0.6 to 0.6
- refl_up: float32 [2, 8192], P('depth', ('row', 'col')), may hold values from -0.6 to 0.6
Outputs:
- down_field: float32 [2, 8192, 256], P('depth', ('row', 'col'))
- up_field: float32 [2, 8192, 256], P('depth', ('row', 'col'))
All inputs are finite; a program needn't handle non-finite values.
Results may differ from a plain program's by a relative error of at most 0.0041.
Values may be sent and summed in bfloat16 or wider, within the bound.
No kernel may reach another device: no remote copies, remote signals or barrier semaphores. Data moves between devices by JAX's collectives and lax.ppermute only.
A program may use at most 64 MiB of HBM per device.

v0:
```python
import jax
import jax.numpy as jnp
from jax import lax
from jax.sharding import PartitionSpec as P

PASSES = 2


def passed_along(x, axis, by):
    peers = lax.axis_size(axis)
    pairs = [(i, i + by) for i in range(peers) if 0 <= i + by < peers]
    return lax.ppermute(x, axis, pairs)


def complex_join(first, second, sources):
    real_part = first[:, :sources] - second[:, sources:]
    imag_part = first[:, sources:] + second[:, :sources]
    return jnp.concatenate([real_part, imag_part], axis=1)


def downward(weight_real, weight_imag, down_low, sources):
    gathered = lax.all_gather(down_low, "row", axis=0, tiled=True)
    return lax.psum_scatter(
        complex_join(
            jnp.dot(weight_real, gathered, preferred_element_type=jnp.float32),
            jnp.dot(weight_imag, gathered, preferred_element_type=jnp.float32),
            sources,
        ),
        "col",
        scatter_dimension=0,
        tiled=True,
    )


def upward(weight_real, weight_imag, up_low, sources):
    gathered = lax.all_gather(up_low, "col", axis=0, tiled=True)
    numbers = (((0,), (0,)), ((), ()))
    first = lax.dot_general(weight_real, gathered, numbers, preferred_element_type=jnp.float32)
    second = lax.dot_general(weight_imag, gathered, numbers, preferred_element_type=jnp.float32)
    return lax.psum_scatter(
        complex_join(first, second, sources), "row", scatter_dimension=0, tiled=True
    )


def send_trans(trans):
    return passed_along(trans, "depth", 1)


def send_back(back):
    return passed_along(back, "depth", -1)


def body(prop, source, down_init, up_init, refl_down, refl_up):
    weight_real = prop[0, 0]
    weight_imag = prop[0, 1]
    sources = down_init.shape[2] // 2
    at_surface = lax.axis_index("depth") == 0
    refl_above = refl_down[0][:, None]
    refl_below = refl_up[0][:, None]
    down = down_init[0]
    up = up_init[0]
    for sweep in range(PASSES):
        down_low = down.astype(jnp.bfloat16)
        up_low = up.astype(jnp.bfloat16)
        trans = downward(weight_real, weight_imag, down_low, sources)
        from_above = send_trans(trans)
        back = upward(weight_real, weight_imag, up_low, sources)
        from_below = send_back(back)
        above = jnp.where(at_surface, source, from_above)
        down = above + refl_above * back
        up = from_below + refl_below * trans
    return (down[None], up[None])


def solution(mesh):
    placed = (
        P("depth", None, "row", "col"),
        P(("row", "col"), None),
        P("depth", ("row", "col"), None),
        P("depth", ("row", "col"), None),
        P("depth", ("row", "col")),
        P("depth", ("row", "col")),
    )
    return jax.shard_map(
        body,
        mesh=mesh,
        in_specs=placed,
        out_specs=(P("depth", ("row", "col"), None), P("depth", ("row", "col"), None)),
        check_vma=False,
    )
```

profile of v0, /device:TPU:0, one launch (start us, length us, event | category | flops | bytes accessed | tf_op | source)
XLA Modules:
  0.0 290.8 jit_solution(9658612321237586070)
XLA Ops:
  7.2 1.8 convert_element_type.18
  9.0 0.0 all-gather.13.cloned.1.call-start
  9.1 1.8 convert_element_type.20
  10.9 0.0 reduce-scatter.5.cloned.1.call-start
  10.9 29.9 %all-gather.11.cloned.1.call-done = bf16[1,2048,256]{2,1,0:T(8,128)(2,1)} async-done(((bf16[1,512,256]{2,1,0:T(8,128)(2,1)}), bf16[1,2048,256]{2,1,0:T(8,128)(2,1)}) %all-gather.11.cloned.1.call-update) | async-done | bytes 1048592 | tf_op jit(solution)/shard_map/all_gather | solution.py:22
  40.8 6.1 %fusion.6 = f32[2048,256]{0,1:T(8,128)S(1)} fusion(bf16[1,2,2048,2048]{3,2,1,0:T(8,128)(2,1)} %param.6, bf16[1,2048,256]{2,1,0:T(8,128)(2,1)} %all-gather.11.cloned.1.call-done), kind=kOutput, calls=%fused_computation.6 | convolution fusion | flops 2147483648 | bytes 11534336 | tf_op jit(solution)/shard_map/dot_general | solution.py:26
  47.0 2.4 copy-done.6
  49.4 0.3 copy-done.10
  49.6 2.4 fusion.14
  52.1 0.3 slice_subtract_fusion.3
  52.3 1.5 pad_maximum_fusion
  53.8 0.0 reduce-scatter.7.cloned.1.call-start
  53.9 5.3 %all-gather.13.cloned.1.call-done = bf16[1,2048,256]{2,1,0:T(8,128)(2,1)} async-done(((bf16[1,512,256]{2,1,0:T(8,128)(2,1)}), bf16[1,2048,256]{2,1,0:T(8,128)(2,1)}) %all-gather.13.cloned.1.call-update) | async-done | bytes 1048592 | tf_op jit(solution)/shard_map/all_gather | solution.py:36
  59.2 6.1 %fusion.4 = f32[2048,256]{0,1:T(8,128)S(1)} fusion(bf16[1,2,2048,2048]{3,2,1,0:T(8,128)(2,1)} %param.6, bf16[1,2048,256]{2,1,0:T(8,128)(2,1)} %all-gather.13.cloned.1.call-done), kind=kOutput, calls=%fused_computation.4 | convolution fusion | flops 2147483648 | bytes 11534336 | tf_op jit(solution)/shard_map/dot_general | solution.py:39
  65.3 6.1 %fusion.12 = f32[2048,256]{0,1:T(8,128)S(1)} fusion(bf16[1,2,2048,2048]{3,2,1,0:T(8,128)(2,1)} %param.6, bf16[1,2048,256]{2,1,0:T(8,128)(2,1)S(1)} %copy-done.7), kind=kOutput, calls=%fused_computation.12 | convolution fusion | flops 2147483648 | bytes 11534336 | tf_op jit(solution)/shard_map/dot_general | solution.py:38
  71.4 0.3 slice_subtract_fusion.2
  71.7 1.5 pad_maximum_fusion.1
  73.2 0.0 all-gather.7.cloned.1.call-start
  73.2 20.0 %reduce-scatter.5.cloned.1.call-done = f32[512,256]{0,1:T(8,128)} async-done(((f32[2048,256]{0,1:T(8,128)}), f32[512,256]{0,1:T(8,128)}) %reduce-scatter.5.cloned.1.call-update) | async-done | bytes 524304 | tf_op jit(solution)/shard_map/reduce_scatter | solution.py:23
  93.2 3.5 %collective-permute-start = (f32[512,256]{0,1:T(8,128)}, f32[512,256]{0,1:T(8,128)S(1)}, u32[]{:S(2)}, u32[]{:S(2)}) collective-permute-start(f32[512,256]{0,1:T(8,128)} %reduce-scatter.5.cloned.1.call-done), channel_id=1, source_target_pairs={{0,16},{1,17},{2,18},{3,19},{4,20},{5,21},{6,22},{7,23},{8,24},{9,... | collective-permute-start | bytes 1572872 | tf_op jit(solution)/shard_map/ppermute | solution.py:12
  96.7 0.2 copy.9
  96.9 42.4 %reduce-scatter.7.cloned.1.call-done = f32[512,256]{0,1:T(8,128)} async-done(((f32[2048,256]{0,1:T(8,128)}), f32[512,256]{0,1:T(8,128)}) %reduce-scatter.7.cloned.1.call-update) | async-done | bytes 524304 | tf_op jit(solution)/shard_map/reduce_scatter | solution.py:40
  139.3 2.0 add_convert_fusion.1
  141.3 0.0 all-gather.9.cloned.1.call-start
  141.4 1.3 collective-permute-start.2
  142.7 14.1 %collective-permute-done.2 = f32[512,256]{0,1:T(8,128)S(1)} collective-permute-done((f32[512,256]{0,1:T(8,128)S(1)}, f32[512,256]{0,1:T(8,128)S(1)}, u32[]{:S(2)}, u32[]{:S(2)}) %collective-permute-start.2) | collective-permute-done | bytes 524320 | tf_op jit(solution)/shard_map/ppermute | solution.py:12
  156.8 0.8 add_convert_fusion
  157.7 0.2 reduce-scatter.9.cloned.1.call-start
  157.9 10.9 %all-gather.7.cloned.1.call-done = bf16[2048,256]{0,1:T(8,128)(2,1)} async-done(((bf16[512,256]{0,1:T(8,128)(2,1)}), bf16[2048,256]{0,1:T(8,128)(2,1)}) %all-gather.7.cloned.1.call-update) | async-done | bytes 1048592 | tf_op jit(solution)/shard_map/all_gather | solution.py:22
  168.8 6.1 %fusion.30 = f32[2048,256]{0,1:T(8,128)S(1)} fusion(bf16[2048,256]{0,1:T(8,128)(2,1)} %all-gather.7.cloned.1.call-done, bf16[1,2,2048,2048]{3,2,1,0:T(8,128)(2,1)} %param.6), kind=kOutput, calls=%fused_computation.26 | convolution fusion | flops 2147483648 | bytes 11534336 | tf_op jit(solution)/shard_map/dot_general | solution.py:26
  174.9 6.1 %fusion.24 = f32[2048,256]{0,1:T(8,128)S(1)} fusion(bf16[2048,256]{0,1:T(8,128)(2,1)S(1)} %copy-done.9, bf16[1,2,2048,2048]{3,2,1,0:T(8,128)(2,1)} %param.6), kind=kOutput, calls=%fused_computation.24 | convolution fusion | flops 2147483648 | bytes 11534336 | tf_op jit(solution)/shard_map/dot_general | solution.py:25
  181.0 0.3 slice_subtract_fusion.1
  181.3 1.5 pad_maximum_fusion.2
  182.8 0.0 reduce-scatter.11.cloned.1.call-start
  182.9 4.1 %all-gather.9.cloned.1.call-done = bf16[2048,256]{0,1:T(8,128)(2,1)} async-done(((bf16[512,256]{0,1:T(8,128)(2,1)}), bf16[2048,256]{0,1:T(8,128)(2,1)}) %all-gather.9.cloned.1.call-update) | async-done | bytes 1048592 | tf_op jit(solution)/shard_map/all_gather | solution.py:36
  187.0 6.1 %fusion.33 = f32[2048,256]{0,1:T(8,128)S(1)} fusion(bf16[2048,256]{0,1:T(8,128)(2,1)} %all-gather.9.cloned.1.call-done, bf16[1,2,2048,2048]{3,2,1,0:T(8,128)(2,1)} %param.6), kind=kOutput, calls=%fused_computation.27 | convolution fusion | flops 2147483648 | bytes 11534336 | tf_op jit(solution)/shard_map/dot_general | solution.py:39
  193.1 6.1 %fusion.27 = f32[2048,256]{0,1:T(8,128)S(1)} fusion(bf16[2048,256]{0,1:T(8,128)(2,1)S(1)} %copy-done.8, bf16[1,2,2048,2048]{3,2,1,0:T(8,128)(2,1)} %param.6), kind=kOutput, calls=%fused_computation.25 | convolution fusion | flops 2147483648 | bytes 11534336 | tf_op jit(solution)/shard_map/dot_general | solution.py:38
  199.3 0.3 slice_subtract_fusion
  199.6 1.5 pad_maximum_fusion.3
  201.1 19.9 %reduce-scatter.9.cloned.1.call-done = f32[512,256]{0,1:T(8,128)} async-done(((f32[2048,256]{0,1:T(8,128)}), f32[512,256]{0,1:T(8,128)}) %reduce-scatter.9.cloned.1.call-update) | async-done | bytes 524304 | tf_op jit(solution)/shard_map/reduce_scatter | solution.py:23
  221.0 3.6 %collective-permute-start.1 = (f32[512,256]{0,1:T(8,128)}, f32[512,256]{0,1:T(8,128)S(1)}, u32[]{:S(2)}, u32[]{:S(2)}) collective-permute-start(f32[512,256]{0,1:T(8,128)} %reduce-scatter.9.cloned.1.call-done), channel_id=1, source_target_pairs={{0,16},{1,17},{2,18},{3,19},{4,20},{5,21},{6,22},{7,23},{8,24},{9,... | collective-permute-start | bytes 1572872 | tf_op jit(solution)/shard_map/ppermute | solution.py:12
  224.6 42.8 %reduce-scatter.11.cloned.1.call-done = f32[512,256]{0,1:T(8,128)} async-done(((f32[2048,256]{0,1:T(8,128)}), f32[512,256]{0,1:T(8,128)}) %reduce-scatter.11.cloned.1.call-update) | async-done | bytes 524304 | tf_op jit(solution)/shard_map/reduce_scatter | solution.py:40
  267.3 1.3 collective-permute-start.3
  268.6 1.2 add_bitcast_fusion.1
  269.8 1.0 copy.10
  270.8 12.1 %collective-permute-done.3 = f32[512,256]{0,1:T(8,128)S(1)} collective-permute-done((f32[512,256]{0,1:T(8,128)}, f32[512,256]{0,1:T(8,128)S(1)}, u32[]{:S(2)}, u32[]{:S(2)}) %collective-permute-start.3) | collective-permute-done | bytes 524320 | tf_op jit(solution)/shard_map/ppermute | solution.py:12
  282.9 0.1 add_bitcast_fusion
  283.0 1.0 copy.11
  (31 shorter events, 0.2 us)
Async XLA Ops:
  7.2 33.6 %all-gather.11.cloned.1.call-start = ((), (), s32[]{:S(2)}) async-start(), calls=%async_computation.10 | async-start | bytes 1310720 | tf_op jit(solution)/shard_map/all_gather | solution.py:22
  9.0 50.2 %all-gather.13.cloned.1.call-start = ((), (), s32[]{:S(2)}) async-start(), calls=%async_computation.11 | async-start | bytes 1310720 | tf_op jit(solution)/shard_map/all_gather | solution.py:36
  10.9 82.3 %reduce-scatter.5.cloned.1.call-start = ((), (), s32[]{:S(2)}) async-start(), calls=%async_computation.4 | async-start | bytes 2621440 | tf_op jit(solution)/shard_map/reduce_scatter | solution.py:23
  40.8 8.6 %copy-start.6 = (bf16[1,2,2048,2048]{3,2,1,0:T(8,128)(2,1)S(1)}, bf16[1,2,2048,2048]{3,2,1,0:T(8,128)(2,1)}, u32[]{:S(2)}) copy-start(bf16[1,2,2048,2048]{3,2,1,0:T(8,128)(2,1)} %param.6) | copy-start | bytes 50331652
  40.8 8.8 %copy-start.10 = (bf16[1,2048,256]{2,1,0:T(8,128)(2,1)S(1)}, bf16[1,2048,256]{2,1,0:T(8,128)(2,1)}, u32[]{:S(2)}) copy-start(bf16[1,2048,256]{2,1,0:T(8,128)(2,1)} %all-gather.11.cloned.1.call-done) | copy-start | bytes 3145732
  53.8 85.5 %reduce-scatter.7.cloned.1.call-start = ((), (), s32[]{:S(2)}) async-start(), calls=%async_computation.5 | async-start | bytes 2621440 | tf_op jit(solution)/shard_map/reduce_scatter | solution.py:40
  59.2 6.1 %copy-start.7 = (bf16[1,2048,256]{2,1,0:T(8,128)(2,1)S(1)}, bf16[1,2048,256]{2,1,0:T(8,128)(2,1)}, u32[]{:S(2)}) copy-start(bf16[1,2048,256]{2,1,0:T(8,128)(2,1)} %all-gather.13.cloned.1.call-done) | copy-start | bytes 3145732
  73.1 23.6 %copy-start.2 = (f32[512,256]{1,0:T(8,128)S(1)}, f32[512,256]{1,0:T(8,128)}, u32[]{:S(2)}) copy-start(f32[512,256]{1,0:T(8,128)} %param.7) | copy-start | bytes 1572868
  73.1 66.2 %copy-start.5 = (f32[1,512]{1,0:T(1,128)S(1)}, f32[1,512]{1,0:T(1,128)}, u32[]{:S(2)}) copy-start(f32[1,512]{1,0:T(1,128)} %param.10) | copy-start | bytes 6148
  73.2 83.7 %copy-start.4 = (f32[1,512]{1,0:T(1,128)S(1)}, f32[1,512]{1,0:T(1,128)}, u32[]{:S(2)}) copy-start(f32[1,512]{1,0:T(1,128)} %param.11) | copy-start | bytes 6148
  73.2 95.6 %all-gather.7.cloned.1.call-start = ((), (), s32[]{:S(2)}) async-start(), calls=%async_computation.6 | async-start | bytes 1310720 | tf_op jit(solution)/shard_map/all_gather | solution.py:22
  93.2 63.6 %copy-start = (f32[512,256]{0,1:T(8,128)S(1)}, f32[512,256]{0,1:T(8,128)}, u32[]{:S(2)}) copy-start(f32[512,256]{0,1:T(8,128)} %reduce-scatter.5.cloned.1.call-done) | copy-start | bytes 1572868
  93.2 46.2 %collective-permute-start = (f32[512,256]{0,1:T(8,128)}, f32[512,256]{0,1:T(8,128)S(1)}, u32[]{:S(2)}, u32[]{:S(2)}) collective-permute-start(f32[512,256]{0,1:T(8,128)} %reduce-scatter.5.cloned.1.call-done), channel_id=1, source_target_pairs={{0,16},{1,17},{2,18},{3,19},{4,20},{5,21},{6,22},{7,23},{8,24},{9,... | collective-permute-start | bytes 1572872 | tf_op jit(solution)/shard_map/ppermute | solution.py:12
  139.3 2.1 copy-start.1
  141.3 45.7 %all-gather.9.cloned.1.call-start = ((), (), s32[]{:S(2)}) async-start(), calls=%async_computation.8 | async-start | bytes 1310720 | tf_op jit(solution)/shard_map/all_gather | solution.py:36
  141.4 15.4 %collective-permute-start.2 = (f32[512,256]{0,1:T(8,128)S(1)}, f32[512,256]{0,1:T(8,128)S(1)}, u32[]{:S(2)}, u32[]{:S(2)}) collective-permute-start(f32[512,256]{0,1:T(8,128)S(1)} %copy-done.1), channel_id=1, source_target_pairs={{16,0},{17,1},{18,2},{19,3},{20,4},{21,5},{22,6},{23,7},{24,8},{25... | collective-permute-start | bytes 1572872 | tf_op jit(solution)/shard_map/ppermute | solution.py:12
  157.7 63.3 %reduce-scatter.9.cloned.1.call-start = ((), (), s32[]{:S(2)}) async-start(), calls=%async_computation.7 | async-start | bytes 2621440 | tf_op jit(solution)/shard_map/reduce_scatter | solution.py:23
  168.8 6.2 %copy-start.9 = (bf16[2048,256]{0,1:T(8,128)(2,1)S(1)}, bf16[2048,256]{0,1:T(8,128)(2,1)}, u32[]{:S(2)}) copy-start(bf16[2048,256]{0,1:T(8,128)(2,1)} %all-gather.7.cloned.1.call-done) | copy-start | bytes 3145732
  182.8 84.5 %reduce-scatter.11.cloned.1.call-start = ((), (), s32[]{:S(2)}) async-start(), calls=%async_computation.9 | async-start | bytes 2621440 | tf_op jit(solution)/shard_map/reduce_scatter | solution.py:40
  187.0 6.1 %copy-start.8 = (bf16[2048,256]{0,1:T(8,128)(2,1)S(1)}, bf16[2048,256]{0,1:T(8,128)(2,1)}, u32[]{:S(2)}) copy-start(bf16[2048,256]{0,1:T(8,128)(2,1)} %all-gather.9.cloned.1.call-done) | copy-start | bytes 3145732
  221.0 61.9 %copy-start.3 = (f32[512,256]{0,1:T(8,128)S(1)}, f32[512,256]{0,1:T(8,128)}, u32[]{:S(2)}) copy-start(f32[512,256]{0,1:T(8,128)} %reduce-scatter.9.cloned.1.call-done) | copy-start | bytes 1572868
  221.0 47.6 %collective-permute-start.1 = (f32[512,256]{0,1:T(8,128)}, f32[512,256]{0,1:T(8,128)S(1)}, u32[]{:S(2)}, u32[]{:S(2)}) collective-permute-start(f32[512,256]{0,1:T(8,128)} %reduce-scatter.9.cloned.1.call-done), channel_id=1, source_target_pairs={{0,16},{1,17},{2,18},{3,19},{4,20},{5,21},{6,22},{7,23},{8,24},{9,... | collective-permute-start | bytes 1572872 | tf_op jit(solution)/shard_map/ppermute | solution.py:12
  267.3 15.6 %collective-permute-start.3 = (f32[512,256]{0,1:T(8,128)}, f32[512,256]{0,1:T(8,128)S(1)}, u32[]{:S(2)}, u32[]{:S(2)}) collective-permute-start(f32[512,256]{0,1:T(8,128)} %reduce-scatter.11.cloned.1.call-done), channel_id=1, source_target_pairs={{16,0},{17,1},{18,2},{19,3},{20,4},{21,5},{22,6},{23,7},{24,8},{25... | collective-permute-start | bytes 1572872 | tf_op jit(solution)/shard_map/ppermute | solution.py:12
Sparse Core Ops, SparseCore 0:
  10.1 30.6 all-gather.10
  42.9 16.2 all-gather.12
  61.7 31.4 reduce-scatter.4
  95.4 43.8 reduce-scatter.6
  141.5 27.2 all-gather.6
  170.8 16.2 all-gather.8
  189.5 31.4 reduce-scatter.8
  223.4 43.8 reduce-scatter.10
where the time goes:
time: 291 us
  waiting for transfers between devices  202 us (69%)
  matrix products  45.2 us (16%)
  other arithmetic  14.6 us (5%)
  between operations  14.3 us (5%)
  starting transfers between devices  10.2 us (4%)
  local copies, waits for them, and re-layouts  4.91 us (2%)
    reduce_scatter x2, waiting for transfers between devices, upward(): lax.psum_scatter(complex_join(first, second, sources), 'row', scatter_dim...  85.2 us
    all_gather x2, waiting for transfers between devices, downward(): gathered = lax.all_gather(down_low, 'row', axis=0, tiled=True)  40.8 us
    reduce_scatter x2, waiting for transfers between devices, downward(): lax.psum_scatter(complex_join(jnp.dot(weight_real, gathered, preferred_el...  39.9 us
    ppermute x4, waiting for transfers between devices, passed_along(): return lax.ppermute(x, axis, pairs)  26.2 us
    dot_general x2, matrix products, downward(): jnp.dot(weight_imag, gathered, preferred_element_type=jnp.float32)  12.3 us
    dot_general x2, matrix products, upward(): lax.dot_general(weight_real, gathered, numbers, preferred_element_type=jn...  12.3 us
    dot_general x2, matrix products, upward(): lax.dot_general(weight_imag, gathered, numbers, preferred_element_type=jn...  12.2 us
    ppermute x4, starting transfers between devices, passed_along(): return lax.ppermute(x, axis, pairs)  9.66 us
  transfers between devices with their start and end apart: 12, of which 10 were waited for; matrix products, arithmetic and copies ran while one was open for 20% of the time, Pallas kernels for 0%

commit v1 on v0

--- a/solution.py
+++ b/solution.py
@@ -4,6 +4,16 @@
 from jax.sharding import PartitionSpec as P
 
 PASSES = 2
+
+
+def turned_line(x, name, d):
+    size = lax.axis_size(name)
+    held, blocks = (x, [x])
+    for _ in range(size - 1):
+        held = lax.ppermute(held, name, [(i, (i + 1) % size) for i in range(size)])
+        blocks.insert(0, held)
+    line = jnp.concatenate(blocks, axis=d)
+    return jnp.roll(line, (lax.axis_index(name) + 1) * x.shape[d], axis=d)
 
 
 def passed_along(x, axis, by):
@@ -33,7 +43,7 @@
 
 
 def upward(weight_real, weight_imag, up_low, sources):
-    gathered = lax.all_gather(up_low, "col", axis=0, tiled=True)
+    gathered = turned_line(up_low, "col", 0)
     numbers = (((0,), (0,)), ((), ()))
     first = lax.dot_general(weight_real, gathered, numbers, preferred_element_type=jnp.float32)
     second = lax.dot_general(weight_imag, gathered, numbers, preferred_element_type=jnp.float32)

time: 291 us -> 281 us (0.966)
  waiting for transfers between devices: 202 us -> 185 us
  other arithmetic: 14.6 us -> 24.1 us
    ppermute x0 -> x6, waiting for transfers between devices: none -> 24.2 us  [turned_line(): held = lax.ppermute(held, name, [(i, (i + 1) % size) for i in range(size)])]
    reduce_scatter x2, waiting for transfers between devices: 85.2 us -> 63.1 us  [upward(): lax.psum_scatter(complex_join(first, second, sources), 'row', scatter_dim...]
    all_gather x2, waiting for transfers between devices: 40.8 us -> 20.1 us  [downward(): gathered = lax.all_gather(down_low, 'row', axis=0, tiled=True)]
    concatenate x0 -> x2, other arithmetic: none -> 10.9 us  [turned_line(): return jnp.roll(line, (lax.axis_index(name) + 1) * x.shape[d], axis=d)]
    reduce_scatter x2, waiting for transfers between devices: 39.9 us -> 49.7 us  [downward(): lax.psum_scatter(complex_join(jnp.dot(weight_real, gathered, preferred_el...]
    all_gather x2 -> x0, waiting for transfers between devices: 9.43 us -> none  [upward(): gathered = lax.all_gather(up_low, 'col', axis=0, tiled=True)]
    dot_general x2, matrix products: 12.3 us -> 8.42 us  [upward(): lax.dot_general(weight_real, gathered, numbers, preferred_element_type=jn...]
    dot_general x2, matrix products: 8.52 us -> 12.3 us  [downward(): jnp.dot(weight_real, gathered, preferred_element_type=jnp.float32)]
  transfers between devices with their start and end apart: 12 -> 16, of which waited for: 10 -> 15; matrix products, arithmetic and copies ran while one was open for 20% -> 24% of each run, Pallas kernels for 0% -> 0%
where the time goes in v1:
time: 281 us
  waiting for transfers between devices  185 us (66%)
  matrix products  44.5 us (16%)
  other arithmetic  24.1 us (9%)
  between operations  14.3 us (5%)
  starting transfers between devices  10.7 us (4%)
    reduce_scatter x2, waiting for transfers between devices, upward(): lax.psum_scatter(complex_join(first, second, sources), 'row', scatter_dim...  63.1 us
    reduce_scatter x2, waiting for transfers between devices, downward(): lax.psum_scatter(complex_join(jnp.dot(weight_real, gathered, preferred_el...  49.7 us
    ppermute x4, waiting for transfers between devices, passed_along(): return lax.ppermute(x, axis, pairs)  27.7 us
    ppermute x6, waiting for transfers between devices, turned_line(): held = lax.ppermute(held, name, [(i, (i + 1) % size) for i in range(size)])  24.2 us
    all_gather x2, waiting for transfers between devices, downward(): gathered = lax.all_gather(down_low, 'row', axis=0, tiled=True)  20.1 us
    dot_general x2, matrix products, downward(): jnp.dot(weight_real, gathered, preferred_element_type=jnp.float32)  12.3 us
    dot_general x2, matrix products, downward(): jnp.dot(weight_imag, gathered, preferred_element_type=jnp.float32)  12.2 us
    dot_general x2, matrix products, upward(): lax.dot_general(weight_imag, gathered, numbers, preferred_element_type=jn...  11.5 us
  transfers between devices with their start and end apart: 16, of which 15 were waited for; matrix products, arithmetic and copies ran while one was open for 24% of the time, Pallas kernels for 0%

profile of v1, /device:TPU:0, one launch (start us, length us, event | category | flops | bytes accessed | tf_op | source)
XLA Modules:
  0.0 280.6 jit_solution(16845856645769185137)
XLA Ops:
  7.2 1.1 convert_bitcast_fusion
  8.3 0.5 collective-permute-start.1
  8.8 6.0 %collective-permute-done.1 = bf16[512,256]{1,0:T(8,128)(2,1)S(1)} collective-permute-done((bf16[512,256]{1,0:T(8,128)(2,1)S(1)}, bf16[512,256]{1,0:T(8,128)(2,1)S(1)}, u32[]{:S(2)}, u32[]{:S(2)}) %collective-permute-start.1) | collective-permute-done | bytes 262176 | tf_op jit(solution)/shard_map/ppermute | solution.py:13
  14.8 5.8 %collective-permute-done.2 = bf16[512,256]{1,0:T(8,128)(2,1)S(1)} collective-permute-done((bf16[512,256]{1,0:T(8,128)(2,1)S(1)}, bf16[512,256]{1,0:T(8,128)(2,1)S(1)}, u32[]{:S(2)}, u32[]{:S(2)}) %collective-permute-start.2) | collective-permute-done | bytes 262176 | tf_op jit(solution)/shard_map/ppermute | solution.py:13
  20.6 1.8 convert_element_type.18
  22.4 3.9 %collective-permute-done.3 = bf16[512,256]{1,0:T(8,128)(2,1)S(1)} collective-permute-done((bf16[512,256]{1,0:T(8,128)(2,1)S(1)}, bf16[512,256]{1,0:T(8,128)(2,1)S(1)}, u32[]{:S(2)}, u32[]{:S(2)}) %collective-permute-start.3) | collective-permute-done | bytes 262176 | tf_op jit(solution)/shard_map/ppermute | solution.py:13
  26.4 9.6 %fusion.52 = bf16[2048,256]{1,0:T(8,128)(2,1)S(1)} fusion(s32[]{:T(128)S(6)} %select_n.28, bf16[512,256]{1,0:T(8,128)(2,1)S(1)} %collective-permute-done.3, bf16[512,256]{1,0:T(8,128)(2,1)S(1)} %collective-permute-done.2, bf16[512,256]{1,0:T(8,128)(2,1)S(1)} %collective-permute-done.1, bf16[512,256]{1,0:T(8,128)(2,1)S(1)} %convert_bitcast_fusion), kind=kLoop, calls=%fused_computation.60 | loop fusion | flops 8388608 | bytes 2097156 | tf_op jit(solution)/shard_map/jit(_roll_dynamic)/concatenate | solution.py:16
  36.0 5.8 %fusion.33 = f32[2048,256]{0,1:T(8,128)S(1)} fusion(bf16[2048,256]{1,0:T(8,128)(2,1)S(1)} %fusion.52, bf16[1,2,2048,2048]{3,2,1,0:T(8,128)(2,1)} %param.8), kind=kOutput, calls=%fused_computation.27 | convolution fusion | flops 2147483648 | bytes 11534336 | tf_op jit(solution)/shard_map/dot_general | solution.py:49
  41.7 2.5 fusion.24
  44.3 0.3 slice_subtract_fusion.2
  44.6 1.5 pad_maximum_fusion.1
  46.2 6.7 %all-gather.6.cloned.1.call-done = bf16[1,2048,256]{2,1,0:T(8,128)(2,1)} async-done(((bf16[1,512,256]{2,1,0:T(8,128)(2,1)}), bf16[1,2048,256]{2,1,0:T(8,128)(2,1)}) %all-gather.6.cloned.1.call-update) | async-done | bytes 1048592 | tf_op jit(solution)/shard_map/all_gather | solution.py:32
  52.8 6.1 %fusion.6 = f32[2048,256]{0,1:T(8,128)S(1)} fusion(bf16[1,2,2048,2048]{3,2,1,0:T(8,128)(2,1)} %param.8, bf16[1,2048,256]{2,1,0:T(8,128)(2,1)} %all-gather.6.cloned.1.call-done), kind=kOutput, calls=%fused_computation.6 | convolution fusion | flops 2147483648 | bytes 11534336 | tf_op jit(solution)/shard_map/dot_general | solution.py:36
  58.9 6.2 %fusion.14 = f32[2048,256]{0,1:T(8,128)S(1)} fusion(bf16[1,2,2048,2048]{3,2,1,0:T(8,128)(2,1)} %param.8, bf16[1,2048,256]{2,1,0:T(8,128)(2,1)S(1)} %copy-done.6), kind=kOutput, calls=%fused_computation.14 | convolution fusion | flops 2147483648 | bytes 11534336 | tf_op jit(solution)/shard_map/dot_general | solution.py:35
  65.1 0.3 slice_subtract_fusion.3
  65.4 1.5 pad_maximum_fusion
  66.9 31.6 %reduce-scatter.7.cloned.1.call-done = f32[512,256]{0,1:T(8,128)} async-done(((f32[2048,256]{0,1:T(8,128)}), f32[512,256]{0,1:T(8,128)}) %reduce-scatter.7.cloned.1.call-update) | async-done | bytes 524304 | tf_op jit(solution)/shard_map/reduce_scatter | solution.py:50
  98.5 1.4 collective-permute-start.5
  99.9 14.3 %collective-permute-done.5 = f32[512,256]{0,1:T(8,128)S(1)} collective-permute-done((f32[512,256]{0,1:T(8,128)}, f32[512,256]{0,1:T(8,128)S(1)}, u32[]{:S(2)}, u32[]{:S(2)}) %collective-permute-start.5) | collective-permute-done | bytes 524320 | tf_op jit(solution)/shard_map/ppermute | solution.py:22
  114.2 17.8 %reduce-scatter.5.cloned.1.call-done = f32[512,256]{0,1:T(8,128)} async-done(((f32[2048,256]{0,1:T(8,128)}), f32[512,256]{0,1:T(8,128)}) %reduce-scatter.5.cloned.1.call-update) | async-done | bytes 524304 | tf_op jit(solution)/shard_map/reduce_scatter | solution.py:33
  132.0 1.1 add_convert_fusion
  133.2 3.4 %collective-permute-start = (f32[512,256]{0,1:T(8,128)}, f32[512,256]{0,1:T(8,128)S(1)}, u32[]{:S(2)}, u32[]{:S(2)}) collective-permute-start(f32[512,256]{0,1:T(8,128)} %reduce-scatter.5.cloned.1.call-done), channel_id=1, source_target_pairs={{0,16},{1,17},{2,18},{3,19},{4,20},{5,21},{6,22},{7,23},{8,24},{9,... | collective-permute-start | bytes 1572872 | tf_op jit(solution)/shard_map/ppermute | solution.py:22
  136.6 2.4 collective-permute-done.6
  139.0 0.2 copy.9
  139.2 5.6 %collective-permute-done.7 = bf16[512,256]{0,1:T(8,128)(2,1)S(1)} collective-permute-done((bf16[512,256]{0,1:T(8,128)(2,1)S(1)}, bf16[512,256]{0,1:T(8,128)(2,1)S(1)}, u32[]{:S(2)}, u32[]{:S(2)}) %collective-permute-start.7) | collective-permute-done | bytes 262176 | tf_op jit(solution)/shard_map/ppermute | solution.py:13
  144.8 4.1 %collective-permute-done = f32[512,256]{0,1:T(8,128)S(1)} collective-permute-done((f32[512,256]{0,1:T(8,128)}, f32[512,256]{0,1:T(8,128)S(1)}, u32[]{:S(2)}, u32[]{:S(2)}) %collective-permute-start) | collective-permute-done | bytes 524320 | tf_op jit(solution)/shard_map/ppermute | solution.py:22
  148.9 0.9 add_convert_fusion.1
  149.8 0.3 reduce-scatter.11.cloned.1.call-start
  150.1 0.5 collective-permute-done.8
  150.6 1.3 fusion.45
  151.9 5.7 %fusion.39 = f32[2048,256]{0,1:T(8,128)S(1)} fusion(bf16[2048,256]{0,1:T(8,128)(2,1)S(1)} %fusion.45, bf16[1,2,2048,2048]{3,2,1,0:T(8,128)(2,1)} %param.8), kind=kOutput, calls=%fused_computation.29 | convolution fusion | flops 2147483648 | bytes 11534336 | tf_op jit(solution)/shard_map/dot_general | solution.py:49
  157.7 5.9 %fusion.30 = f32[2048,256]{0,1:T(8,128)S(1)} fusion(bf16[2048,256]{0,1:T(8,128)(2,1)S(1)} %fusion.45, bf16[1,2,2048,2048]{3,2,1,0:T(8,128)(2,1)} %param.8), kind=kOutput, calls=%fused_computation.26 | convolution fusion | flops 2147483648 | bytes 11534336 | tf_op jit(solution)/shard_map/dot_general | solution.py:48
  163.6 0.3 slice_subtract_fusion
  163.9 1.5 pad_maximum_fusion.3
  165.4 13.4 %all-gather.4.cloned.1.call-done = bf16[2048,256]{0,1:T(8,128)(2,1)} async-done(((bf16[512,256]{0,1:T(8,128)(2,1)}), bf16[2048,256]{0,1:T(8,128)(2,1)}) %all-gather.4.cloned.1.call-update) | async-done | bytes 1048592 | tf_op jit(solution)/shard_map/all_gather | solution.py:32
  178.9 6.1 %fusion.36 = f32[2048,256]{0,1:T(8,128)S(1)} fusion(bf16[2048,256]{0,1:T(8,128)(2,1)} %all-gather.4.cloned.1.call-done, bf16[1,2,2048,2048]{3,2,1,0:T(8,128)(2,1)} %param.8), kind=kOutput, calls=%fused_computation.28 | convolution fusion | flops 2147483648 | bytes 11534336 | tf_op jit(solution)/shard_map/dot_general | solution.py:36
  185.0 6.1 %fusion.27 = f32[2048,256]{0,1:T(8,128)S(1)} fusion(bf16[2048,256]{0,1:T(8,128)(2,1)S(1)} %copy-done.7, bf16[1,2,2048,2048]{3,2,1,0:T(8,128)(2,1)} %param.8), kind=kOutput, calls=%fused_computation.25 | convolution fusion | flops 2147483648 | bytes 11534336 | tf_op jit(solution)/shard_map/dot_general | solution.py:35
  191.2 0.3 slice_subtract_fusion.1
  191.5 1.5 pad_maximum_fusion.2
  192.9 31.5 %reduce-scatter.11.cloned.1.call-done = f32[512,256]{0,1:T(8,128)} async-done(((f32[2048,256]{0,1:T(8,128)}), f32[512,256]{0,1:T(8,128)}) %reduce-scatter.11.cloned.1.call-update) | async-done | bytes 524304 | tf_op jit(solution)/shard_map/reduce_scatter | solution.py:50
  224.4 1.4 collective-permute-start.9
  225.8 31.9 %reduce-scatter.9.cloned.1.call-done = f32[512,256]{0,1:T(8,128)} async-done(((f32[2048,256]{0,1:T(8,128)}), f32[512,256]{0,1:T(8,128)}) %reduce-scatter.9.cloned.1.call-update) | async-done | bytes 524304 | tf_op jit(solution)/shard_map/reduce_scatter | solution.py:33
  257.7 3.4 %collective-permute-start.4 = (f32[512,256]{0,1:T(8,128)}, f32[512,256]{0,1:T(8,128)S(1)}, u32[]{:S(2)}, u32[]{:S(2)}) collective-permute-start(f32[512,256]{0,1:T(8,128)} %reduce-scatter.9.cloned.1.call-done), channel_id=1, source_target_pairs={{0,16},{1,17},{2,18},{3,19},{4,20},{5,21},{6,22},{7,23},{8,24},{9,... | collective-permute-start | bytes 1572872 | tf_op jit(solution)/shard_map/ppermute | solution.py:22
  261.2 1.1 add_bitcast_fusion
  262.3 1.0 copy.11
  263.3 9.3 %collective-permute-done.4 = f32[512,256]{0,1:T(8,128)S(1)} collective-permute-done((f32[512,256]{0,1:T(8,128)}, f32[512,256]{0,1:T(8,128)S(1)}, u32[]{:S(2)}, u32[]{:S(2)}) %collective-permute-start.4) | collective-permute-done | bytes 524320 | tf_op jit(solution)/shard_map/ppermute | solution.py:22
  272.6 0.2 add_bitcast_fusion.1
  272.8 1.0 copy.10
  (33 shorter events, 0.4 us)
Async XLA Ops:
  7.2 45.7 %all-gather.6.cloned.1.call-start = ((), (), s32[]{:S(2)}) async-start(), calls=%async_computation.9 | async-start | bytes 1310720 | tf_op jit(solution)/shard_map/all_gather | solution.py:32
  8.3 6.5 %collective-permute-start.1 = (bf16[512,256]{1,0:T(8,128)(2,1)S(1)}, bf16[512,256]{1,0:T(8,128)(2,1)S(1)}, u32[]{:S(2)}, u32[]{:S(2)}) collective-permute-start(bf16[512,256]{1,0:T(8,128)(2,1)S(1)} %convert_bitcast_fusion), channel_id=1, source_target_pairs={{0,1},{1,2},{2,3},{3,0},{4,5},{5,6},{6,7},{7,4},{8,9},{9,10},{10,1... | collective-permute-start | bytes 786440 | tf_op jit(solution)/shard_map/ppermute | solution.py:13
  14.8 5.8 %collective-permute-start.2 = (bf16[512,256]{1,0:T(8,128)(2,1)S(1)}, bf16[512,256]{1,0:T(8,128)(2,1)S(1)}, u32[]{:S(2)}, u32[]{:S(2)}) collective-permute-start(bf16[512,256]{1,0:T(8,128)(2,1)S(1)} %collective-permute-done.1), channel_id=1, source_target_pairs={{0,1},{1,2},{2,3},{3,0},{4,5},{5,6},{6,7},{7,4},{8,9},{9,10},{10,1... | collective-permute-start | bytes 786440 | tf_op jit(solution)/shard_map/ppermute | solution.py:13
  20.6 5.8 %collective-permute-start.3 = (bf16[512,256]{1,0:T(8,128)(2,1)S(1)}, bf16[512,256]{1,0:T(8,128)(2,1)S(1)}, u32[]{:S(2)}, u32[]{:S(2)}) collective-permute-start(bf16[512,256]{1,0:T(8,128)(2,1)S(1)} %collective-permute-done.2), channel_id=1, source_target_pairs={{0,1},{1,2},{2,3},{3,0},{4,5},{5,6},{6,7},{7,4},{8,9},{9,10},{10,1... | collective-permute-start | bytes 786440 | tf_op jit(solution)/shard_map/ppermute | solution.py:13
  22.4 76.2 %reduce-scatter.7.cloned.1.call-start = ((), (), s32[]{:S(2)}) async-start(), calls=%async_computation.5 | async-start | bytes 2621440 | tf_op jit(solution)/shard_map/reduce_scatter | solution.py:50
  26.4 15.4 %copy-start.5 = (bf16[1,2,2048,2048]{3,2,1,0:T(8,128)(2,1)S(1)}, bf16[1,2,2048,2048]{3,2,1,0:T(8,128)(2,1)}, u32[]{:S(2)}) copy-start(bf16[1,2,2048,2048]{3,2,1,0:T(8,128)(2,1)} %param.8) | copy-start | bytes 50331652
  46.1 85.9 %reduce-scatter.5.cloned.1.call-start = ((), (), s32[]{:S(2)}) async-start(), calls=%async_computation.4 | async-start | bytes 2621440 | tf_op jit(solution)/shard_map/reduce_scatter | solution.py:33
  52.8 6.1 %copy-start.6 = (bf16[1,2048,256]{2,1,0:T(8,128)(2,1)S(1)}, bf16[1,2048,256]{2,1,0:T(8,128)(2,1)}, u32[]{:S(2)}) copy-start(bf16[1,2048,256]{2,1,0:T(8,128)(2,1)} %all-gather.6.cloned.1.call-done) | copy-start | bytes 3145732
  66.8 65.2 %copy-start.3 = (f32[1,512]{1,0:T(1,128)S(1)}, f32[1,512]{1,0:T(1,128)}, u32[]{:S(2)}) copy-start(f32[1,512]{1,0:T(1,128)} %param.13) | copy-start | bytes 6148
  66.8 72.2 %copy-start.1 = (f32[512,256]{1,0:T(8,128)S(1)}, f32[512,256]{1,0:T(8,128)}, u32[]{:S(2)}) copy-start(f32[512,256]{1,0:T(8,128)} %param.9) | copy-start | bytes 1572868
  66.8 82.1 %copy-start.4 = (f32[1,512]{1,0:T(1,128)S(1)}, f32[1,512]{1,0:T(1,128)}, u32[]{:S(2)}) copy-start(f32[1,512]{1,0:T(1,128)} %param.12) | copy-start | bytes 6148
  66.8 112.0 %all-gather.4.cloned.1.call-start = ((), (), s32[]{:S(2)}) async-start(), calls=%async_computation.6 | async-start | bytes 1310720 | tf_op jit(solution)/shard_map/all_gather | solution.py:32
  98.5 50.4 %copy-start = (f32[512,256]{0,1:T(8,128)S(1)}, f32[512,256]{0,1:T(8,128)}, u32[]{:S(2)}) copy-start(f32[512,256]{0,1:T(8,128)} %reduce-scatter.7.cloned.1.call-done) | copy-start | bytes 1572868
  98.5 15.7 %collective-permute-start.5 = (f32[512,256]{0,1:T(8,128)}, f32[512,256]{0,1:T(8,128)S(1)}, u32[]{:S(2)}, u32[]{:S(2)}) collective-permute-start(f32[512,256]{0,1:T(8,128)} %reduce-scatter.7.cloned.1.call-done), channel_id=1, source_target_pairs={{16,0},{17,1},{18,2},{19,3},{20,4},{21,5},{22,6},{23,7},{24,8},{25... | collective-permute-start | bytes 1572872 | tf_op jit(solution)/shard_map/ppermute | solution.py:22
  133.2 5.8 %collective-permute-start.6 = (bf16[512,256]{0,1:T(8,128)(2,1)S(1)}, bf16[512,256]{0,1:T(8,128)(2,1)S(1)}, u32[]{:S(2)}, u32[]{:S(2)}) collective-permute-start(bf16[512,256]{0,1:T(8,128)(2,1)S(1)} %add_convert_fusion), channel_id=1, source_target_pairs={{0,1},{1,2},{2,3},{3,0},{4,5},{5,6},{6,7},{7,4},{8,9},{9,10},{10,1... | collective-permute-start | bytes 786440 | tf_op jit(solution)/shard_map/ppermute | solution.py:13
  133.2 15.7 %collective-permute-start = (f32[512,256]{0,1:T(8,128)}, f32[512,256]{0,1:T(8,128)S(1)}, u32[]{:S(2)}, u32[]{:S(2)}) collective-permute-start(f32[512,256]{0,1:T(8,128)} %reduce-scatter.5.cloned.1.call-done), channel_id=1, source_target_pairs={{0,16},{1,17},{2,18},{3,19},{4,20},{5,21},{6,22},{7,23},{8,24},{9,... | collective-permute-start | bytes 1572872 | tf_op jit(solution)/shard_map/ppermute | solution.py:22
  139.0 5.8 %collective-permute-start.7 = (bf16[512,256]{0,1:T(8,128)(2,1)S(1)}, bf16[512,256]{0,1:T(8,128)(2,1)S(1)}, u32[]{:S(2)}, u32[]{:S(2)}) collective-permute-start(bf16[512,256]{0,1:T(8,128)(2,1)S(1)} %collective-permute-done.6), channel_id=1, source_target_pairs={{0,1},{1,2},{2,3},{3,0},{4,5},{5,6},{6,7},{7,4},{8,9},{9,10},{10,1... | collective-permute-start | bytes 786440 | tf_op jit(solution)/shard_map/ppermute | solution.py:13
  144.8 5.8 %collective-permute-start.8 = (bf16[512,256]{0,1:T(8,128)(2,1)S(1)}, bf16[512,256]{0,1:T(8,128)(2,1)S(1)}, u32[]{:S(2)}, u32[]{:S(2)}) collective-permute-start(bf16[512,256]{0,1:T(8,128)(2,1)S(1)} %collective-permute-done.7), channel_id=1, source_target_pairs={{0,1},{1,2},{2,3},{3,0},{4,5},{5,6},{6,7},{7,4},{8,9},{9,10},{10,1... | collective-permute-start | bytes 786440 | tf_op jit(solution)/shard_map/ppermute | solution.py:13
  149.8 74.6 %reduce-scatter.11.cloned.1.call-start = ((), (), s32[]{:S(2)}) async-start(), calls=%async_computation.8 | async-start | bytes 2621440 | tf_op jit(solution)/shard_map/reduce_scatter | solution.py:50
  165.4 92.4 %reduce-scatter.9.cloned.1.call-start = ((), (), s32[]{:S(2)}) async-start(), calls=%async_computation.7 | async-start | bytes 2621440 | tf_op jit(solution)/shard_map/reduce_scatter | solution.py:33
  178.9 6.2 %copy-start.7 = (bf16[2048,256]{0,1:T(8,128)(2,1)S(1)}, bf16[2048,256]{0,1:T(8,128)(2,1)}, u32[]{:S(2)}) copy-start(bf16[2048,256]{0,1:T(8,128)(2,1)} %all-gather.4.cloned.1.call-done) | copy-start | bytes 3145732
  224.4 48.2 %copy-start.2 = (f32[512,256]{0,1:T(8,128)S(1)}, f32[512,256]{0,1:T(8,128)}, u32[]{:S(2)}) copy-start(f32[512,256]{0,1:T(8,128)} %reduce-scatter.11.cloned.1.call-done) | copy-start | bytes 1572868
  224.4 36.7 %collective-permute-start.9 = (f32[512,256]{0,1:T(8,128)}, f32[512,256]{0,1:T(8,128)S(1)}, u32[]{:S(2)}, u32[]{:S(2)}) collective-permute-start(f32[512,256]{0,1:T(8,128)} %reduce-scatter.11.cloned.1.call-done), channel_id=1, source_target_pairs={{16,0},{17,1},{18,2},{19,3},{20,4},{21,5},{22,6},{23,7},{24,8},{25... | collective-permute-start | bytes 1572872 | tf_op jit(solution)/shard_map/ppermute | solution.py:22
  257.7 14.9 %collective-permute-start.4 = (f32[512,256]{0,1:T(8,128)}, f32[512,256]{0,1:T(8,128)S(1)}, u32[]{:S(2)}, u32[]{:S(2)}) collective-permute-start(f32[512,256]{0,1:T(8,128)} %reduce-scatter.9.cloned.1.call-done), channel_id=1, source_target_pairs={{0,16},{1,17},{2,18},{3,19},{4,20},{5,21},{6,22},{7,23},{8,24},{9,... | collective-permute-start | bytes 1572872 | tf_op jit(solution)/shard_map/ppermute | solution.py:22
Sparse Core Ops, SparseCore 0:
  22.5 30.3 all-gather.5
  55.1 43.3 reduce-scatter.6
  101.2 30.7 reduce-scatter.4
  149.9 28.9 all-gather.3
  181.0 43.3 reduce-scatter.10
  227.0 30.7 reduce-scatter.8
